TPU v7x, 32 devices: a whole 2x2x4 slice. The times are simulated.
32 devices in a mesh: grp: 2 (over x), seq: 8 (over z, y), ch: 2 (over core).
Axes of the slice: x: 2, y: 2, z: 4, core: 2. Of those that a mesh axis runs over, the one named last changes fastest.
Arguments:
- seq_in: bfloat16 [4096, 1536], P(('grp', 'seq'), 'ch'), parts along dimension 0, may hold values from -6 to 6
- conv_gain: float32 [2, 1536], P(None, 'ch'), may hold values from 0.5 to 1.5
- dw_kernel: float32 [2, 5, 1536], P(None, None, 'ch'), may hold values from -2.5 to 2.5
- mix_weight: bfloat16 [2, 1536, 1536], P(None, 'ch'), may hold values from -0.15625 to 0.15625
- attn_gain: float32 [1536], P('ch'), may hold values from 0.8 to 100, as said below
- q_weight: bfloat16 [1536, 1024], P(None, 'ch'), may hold values from -0.15625 to 0.15625
- kv_weight: bfloat16 [1536, 2, 256], P(None, None, 'ch'), may hold values from -0.15625 to 0.15625
- out_weight: bfloat16 [1024, 1536], P('ch'), may hold values from -0.1875 to 0.1875
Outputs:
- seq_out: bfloat16 [4096, 1536], P(('grp', 'seq'), 'ch'), parts along dimension 0
There are 2 independent parts, one for each index of `grp`. A program takes and returns all parts, laid end to end along the dimension named above; an argument that names none is the same for every part. Nothing has to cross between parts.
Inputs may be any that keep to these rules, and one draw needn't show every extreme that they name: `attn_gain`: gains of the attention norm are positive.
All inputs are finite; a program needn't handle non-finite values.
Results may differ from a plain program's by a relative error of at most 0.03.
The roundings to bfloat16 on the way count: a program that leaves them out, or rounds other values in their place, can miss the bound.
Values may be sent and summed in bfloat16 or wider, within the bound.
No kernel may reach another device: no remote copies, remote signals or barrier semaphores. Data moves between devices by JAX's collectives and lax.ppermute only.
A program may use at most 64 MiB of HBM per device.

v0:
```python
import math
import jax
import jax.numpy as jnp
from jax import lax
from jax.sharding import PartitionSpec as P

HD = 128
EPSILON = 1e-06


def extended(shard, sides, width):
    for axis, dim in sides:
        size, length = (lax.axis_size(axis), shard.shape[dim])
        up = [(i, (i + 1) % size) for i in range(size - 1)]
        down = [(j, i) for i, j in up]
        last = lax.slice_in_dim(shard, length - width, length, axis=dim)
        initial = lax.slice_in_dim(shard, 0, width, axis=dim)
        before = lax.ppermute(last, axis, up)
        after = lax.ppermute(initial, axis, down)
        shard = jnp.concatenate([before, shard, after], axis=dim)
    return shard


def row_normalize(hidden, gain):
    channels = hidden.shape[1] * lax.axis_size("ch")
    squares = lax.psum(jnp.sum(hidden * hidden, axis=1), "ch")
    return hidden * lax.rsqrt(squares[:, None] / channels + EPSILON) * gain


def dilated_sum(padded, kernels, dilation, row_count):
    summed = padded[0:row_count] * kernels[0]
    for tap_index in range(1, kernels.shape[0]):
        summed = (
            summed
            + padded[tap_index * dilation : tap_index * dilation + row_count] * kernels[tap_index]
        )
    return summed


def channel_mix(gelu_output, weight):
    return lax.psum_scatter(
        jnp.dot(gelu_output, weight, preferred_element_type=jnp.float32),
        "ch",
        scatter_dimension=1,
        tiled=True,
    )


def local(seq_in, conv_gain, dw_kernel, mix_weight, attn_gain, q_weight, kv_weight, out_weight):
    local_rows = seq_in.shape[0]
    kernel_half = dw_kernel.shape[1] // 2
    dilation_list = [local_rows // 8, local_rows // 4]
    first_reach = kernel_half * dilation_list[0]
    second_reach = kernel_half * dilation_list[1]
    widened = extended(seq_in, (("seq", 0),), first_reach + second_reach).astype(jnp.float32)
    normalized_rows = row_normalize(widened, conv_gain[0])
    leading_rows = local_rows + 2 * second_reach
    summed = dilated_sum(normalized_rows, dw_kernel[0], dilation_list[0], leading_rows)
    gelu_output = jax.nn.gelu(summed, approximate=True).astype(jnp.bfloat16)
    middle = widened[first_reach : first_reach + leading_rows] + channel_mix(
        gelu_output, mix_weight[0]
    )
    position = (
        lax.axis_index("seq") * local_rows
        - second_reach
        + lax.broadcasted_iota(jnp.int32, (leading_rows,), 0)
    )
    inside = (position >= 0) & (position < local_rows * lax.axis_size("seq"))
    middle = jnp.where(inside[:, None], middle, 0.0)
    normalized_rows = row_normalize(middle, conv_gain[1])
    summed = dilated_sum(normalized_rows, dw_kernel[1], dilation_list[1], local_rows)
    gelu_output = jax.nn.gelu(summed, approximate=True).astype(jnp.bfloat16)
    hidden = middle[second_reach : second_reach + local_rows] + channel_mix(
        gelu_output, mix_weight[1]
    )
    normalized_rows = row_normalize(hidden, attn_gain).astype(jnp.bfloat16)
    features = lax.all_gather(normalized_rows, "ch", axis=1, tiled=True)
    query_rows = jnp.dot(features, q_weight, preferred_element_type=jnp.float32).astype(
        jnp.bfloat16
    )
    kv_width = kv_weight.shape[2]
    pairs = jnp.dot(
        features,
        kv_weight.reshape(kv_weight.shape[0], 2 * kv_width),
        preferred_element_type=jnp.float32,
    ).astype(jnp.bfloat16)
    keys_local = pairs[:, :kv_width]
    values_local = pairs[:, kv_width:]
    kv_local = kv_width // HD
    group_size = q_weight.shape[1] // HD // kv_local
    query_grid = query_rows.reshape(local_rows, kv_local, group_size, HD)
    scale = 1.0 / math.sqrt(HD)

    def key_block(carry, block):
        running_max, running_sum, context = carry
        key_part, value_part = block
        scores = (
            jnp.einsum("pkgd,skd->kgps", query_grid, key_part, preferred_element_type=jnp.float32)
            * scale
        )
        new_max = jnp.maximum(running_max, jnp.max(scores, axis=-1))
        factor = jnp.exp(running_max - new_max)
        probs = jnp.exp(scores - new_max[..., None])
        running_sum = running_sum * factor + jnp.sum(probs, axis=-1)
        update = jnp.einsum(
            "kgps,skd->kgpd",
            probs.astype(jnp.bfloat16),
            value_part,
            preferred_element_type=jnp.float32,
        )
        context = context * factor[..., None] + update
        return ((new_max, running_sum, context), None)

    initial = (
        jnp.full((kv_local, group_size, local_rows), -1e30, jnp.float32),
        jnp.zeros((kv_local, group_size, local_rows), jnp.float32),
        jnp.zeros((kv_local, group_size, local_rows, HD), jnp.float32),
    )
    carry = initial
    key_piece = lax.all_gather(keys_local, "seq", axis=0, tiled=True)
    value_piece = lax.all_gather(values_local, "seq", axis=0, tiled=True)
    key_count = key_piece.shape[0]
    block_len = math.gcd(key_count, 512)
    blocks = (
        key_piece.reshape(key_count // block_len, block_len, kv_local, HD),
        value_piece.reshape(key_count // block_len, block_len, kv_local, HD),
    )
    carry, unused = lax.scan(key_block, carry, blocks)
    running_max, running_sum, context = carry
    attended = (context / running_sum[..., None]).astype(jnp.bfloat16)
    attended = jnp.transpose(attended, (2, 0, 1, 3)).reshape(local_rows, kv_local * group_size * HD)
    mixed = lax.psum_scatter(
        jnp.dot(attended, out_weight, preferred_element_type=jnp.float32).astype(jnp.bfloat16),
        "ch",
        scatter_dimension=1,
        tiled=True,
    ).astype(jnp.float32)
    return (hidden + mixed).astype(jnp.bfloat16)


def solution(mesh):
    return jax.shard_map(
        local,
        mesh=mesh,
        in_specs=(
            P(("grp", "seq"), "ch"),
            P(None, "ch"),
            P(None, None, "ch"),
            P(None, "ch", None),
            P("ch"),
            P(None, "ch"),
            P(None, None, "ch"),
            P("ch", None),
        ),
        out_specs=P(("grp", "seq"), "ch"),
        check_vma=False,
    )
```

profile of v0, /device:TPU:0, one launch (start us, length us, event | category | flops | bytes accessed | tf_op | source)
XLA Modules:
  0.0 192.6 jit_solution(12931244962817168558)
XLA Ops:
  6.5 1.2 fusion.83
  7.8 4.9 %collective-permute-start = (bf16[192,768]{1,0:T(8,128)(2,1)S(1)}, bf16[192,768]{1,0:T(8,128)(2,1)S(1)}, u32[]{:S(2)}, u32[]{:S(2)}) collective-permute-start(bf16[192,768]{1,0:T(8,128)(2,1)S(1)} %get-tuple-element.115), channel_id=1, source_target_pairs={{0,2},{2,4},{4,6},{6,8},{8,10},{10,12},{12,14},{1,3},{3,5},{5,7},{... | collective-permute-start | bytes 884744 | tf_op jit(solution)/shard_map/ppermute | solution.py:18
  12.7 1.3 collective-permute-start.1
  14.0 0.8 slice_reduce_fusion.5
  14.8 0.9 slice_reduce_fusion.4
  15.7 9.5 %collective-permute-done = bf16[192,768]{1,0:T(8,128)(2,1)S(1)} collective-permute-done((bf16[192,768]{1,0:T(8,128)(2,1)S(1)}, bf16[192,768]{1,0:T(8,128)(2,1)S(1)}, u32[]{:S(2)}, u32[]{:S(2)}) %collective-permute-start) | collective-permute-done | bytes 294944 | tf_op jit(solution)/shard_map/ppermute | solution.py:18
  25.2 1.3 multiply_reduce_fusion
  26.5 2.5 %psum.21 = f32[640]{0:T(1024)S(1)} all-reduce(f32[640]{0:T(1024)S(1)} %multiply_reduce_fusion), channel_id=1, replica_groups=mesh['grp'=2,'seq'=8,'ch'=2] {'ch'}, use_global_device_ids=true, to_apply=%region_1.0 | all-reduce | flops 640 | bytes 5120 | tf_op jit(solution)/shard_map/psum | solution.py:26
  29.0 0.3 multiply_multiply_fusion.1
  29.2 5.3 %fusion.20 = f32[512,1536]{1,0:T(8,128)} fusion(bf16[2,768,1536]{2,1,0:T(8,128)(2,1)} %param.13, f32[640,768]{1,0:T(8,128)S(1)} %multiply_multiply_fusion.1, f32[768]{0:T(1024)S(1)} %get-tuple-element.86, f32[768]{0:T(1024)S(1)} %get-tuple-element.87, f32[768]{0:T(1024)S(1)} %get-tuple-element.88, f32[768]{0:T(1024)S(1)} %get-tuple-element.89, ...), kind=kOutput, calls=%fused_computation.29 | convolution fusion | flops 1215037440 | bytes 13389824 | tf_op jit(solution)/shard_map/dot_general | solution.py:42
  34.5 0.0 reduce-scatter.4.cloned.1.call-update
  34.6 0.0 reduce-scatter.6.cloned.1.call-start
  34.6 1.4 maximum_convert_fusion
  36.1 11.7 %reduce-scatter.4.cloned.1.call-done = f32[512,768]{1,0:T(8,128)} async-done(((f32[512,1536]{1,0:T(8,128)}), f32[512,768]{1,0:T(8,128)}) %reduce-scatter.4.cloned.1.call-update) | async-done | bytes 1572880 | tf_op jit(solution)/shard_map/reduce_scatter | solution.py:41
  47.8 2.2 %multiply_reduce_fusion.1 = (f32[512]{0:T(512)S(1)}, f32[512,768]{1,0:T(8,128)S(1)}) fusion(f32[512,768]{1,0:T(8,128)} %reduce-scatter.4.cloned.1.call-done, f32[640,768]{1,0:T(8,128)} %maximum_convert_fusion, pred[512]{0:T(512)(128)(4,1)S(1)} %fusion.73), kind=kLoop, calls=%fused_computation.55 | loop fusion | flops 1572352 | bytes 4721152 | tf_op jit(solution)/shard_map/reduce_sum | solution.py:26
  50.0 2.5 %psum.22 = f32[512]{0:T(512)S(1)} all-reduce(f32[512]{0:T(512)S(1)} %get-tuple-element.111), channel_id=1, replica_groups=mesh['grp'=2,'seq'=8,'ch'=2] {'ch'}, use_global_device_ids=true, to_apply=%region_4.5 | all-reduce | flops 512 | bytes 4096 | tf_op jit(solution)/shard_map/psum | solution.py:26
  52.5 0.2 multiply_multiply_fusion.2
  52.7 3.9 %fusion.18 = f32[256,1536]{1,0:T(8,128)} fusion(bf16[2,768,1536]{2,1,0:T(8,128)(2,1)} %param.13, f32[512,768]{1,0:T(8,128)S(1)} %multiply_multiply_fusion.2, f32[768]{0:T(1024)S(1)} %get-tuple-element.91, f32[768]{0:T(1024)S(1)} %get-tuple-element.92, f32[768]{0:T(1024)S(1)} %get-tuple-element.84, f32[768]{0:T(1024)S(1)} %get-tuple-element.85, ...), kind=kOutput, calls=%fused_computation.27 | convolution fusion | flops 607518720 | bytes 7884800 | tf_op jit(solution)/shard_map/dot_general | solution.py:42
  56.6 0.0 reduce-scatter.8.cloned.1.call-start
  56.7 10.3 %reduce-scatter.6.cloned.1.call-done = f32[256,768]{1,0:T(8,128)} async-done(((f32[256,1536]{1,0:T(8,128)}), f32[256,768]{1,0:T(8,128)}) %reduce-scatter.6.cloned.1.call-update) | async-done | bytes 786448 | tf_op jit(solution)/shard_map/reduce_scatter | solution.py:41
  67.0 1.3 multiply_reduce_fusion.2
  68.3 2.5 %psum.23 = f32[256]{0:T(256)S(1)} all-reduce(f32[256]{0:T(256)S(1)} %multiply_reduce_fusion.2), channel_id=1, replica_groups=mesh['grp'=2,'seq'=8,'ch'=2] {'ch'}, use_global_device_ids=true, to_apply=%region_7.8 | all-reduce | flops 256 | bytes 2048 | tf_op jit(solution)/shard_map/psum | solution.py:26
  70.8 1.3 multiply_convert_fusion
  72.1 2.4 %all_gather.9 = bf16[256,1536]{1,0:T(8,128)(2,1)S(1)} all-gather(bf16[256,768]{1,0:T(8,128)(2,1)S(1)} %multiply_convert_fusion), channel_id=1, replica_groups=mesh['grp'=2,'seq'=8,'ch'=2] {'ch'}, dimensions={1}, use_global_device_ids=true | all-gather | bytes 1179648 | tf_op jit(solution)/shard_map/all_gather | solution.py:77
  74.5 0.4 convolution_convert_fusion.2
  74.9 33.7 %all_gather.10 = bf16[2048,128]{1,0:T(8,128)(2,1)} all-gather(bf16[256,128]{1,0:T(8,128)(2,1)S(1)} %get-tuple-element.118), channel_id=1, replica_groups=mesh['grp'=2,'seq'=8,'ch'=2] {'seq'}, dimensions={0}, use_global_device_ids=true | all-gather | bytes 589824 | tf_op jit(solution)/shard_map/all_gather | solution.py:120
  108.6 33.4 %all_gather.11 = bf16[2048,128]{1,0:T(8,128)(2,1)} all-gather(bf16[256,128]{1,0:T(8,128)(2,1)S(1)} %get-tuple-element.117), channel_id=1, replica_groups=mesh['grp'=2,'seq'=8,'ch'=2] {'seq'}, dimensions={0}, use_global_device_ids=true | all-gather | bytes 589824 | tf_op jit(solution)/shard_map/all_gather | solution.py:121
  142.0 0.6 convolution_convert_fusion.1
  142.6 0.8 reshape.86
  143.3 1.0 copy.15
  144.3 25.2 %while.15 = (s32[]{:T(128)}, f32[1,4,256]{2,1,0:T(4,128)S(1)}, f32[1,4,256]{2,1,0:T(4,128)S(1)}, f32[1,4,256,128]{3,2,1,0:T(8,128)}, bf16[4,512,1,128]{3,1,2,0:T...) while((s32[]{:T(128)}, f32[1,4,256]{2,1,0:T(4,128)S(1)}, ...), condition=%wide.region_11.12_spmd.clone, body=%wide.region_8.11_spmd.clone.sunk | while | flops 273029120 | bytes 16319621 | solution.py:128
  144.3 2.7 %bitcast_reduce_fusion.2 = (f32[4,256]{1,0:T(4,128)S(1)}, f32[512,256,4]{1,0,2:T(8,128)}) fusion(bf16[256,1,4,128]{3,0,2,1:T(8,128)(2,1)S(1)} %get-tuple-element.193, bf16[4,512,1,128]{3,1,2,0:T(8,128)(2,1)} %get-tuple-element.192, s32[]{:T(128)} %get-tuple-element.179), kind=kOutput, calls=%fused_computation.1.clone.1 | convolution fusion | flops 135265280 | bytes 2494976 | tf_op jit(solution)/shard_map/while/body/eval_jaxpr/pkgd,skd->kgps/dot_general | solution.py:98
  147.1 3.1 %fusion.99 = f32[1,4,256,128]{3,2,1,0:T(8,128)} fusion(f32[512,256,4]{1,0,2:T(8,128)} %get-tuple-element.168, f32[4,256]{1,0:T(4,128)S(1)} %bitcast.95, f32[1,4,256,128]{3,2,1,0:T(8,128)} %get-tuple-element.182, f32[4,256]{1,0:T(4,128)S(1)} %get-tuple-element.169, pred[]{:T(512)S(6)} %compare.3, bf16[4,512,1,128]{3,1,2,0:T(8,128)(2,1)} %get-tuple-element.194, ...), kind=kOutput, calls=%fused_computation.6.clone.1 | convolution fusion | flops 136183808 | bytes 3285505 | tf_op jit(solution)/shard_map/while/body/eval_jaxpr/kgps,skd->kgpd/dot_general | solution.py:105
  150.1 0.4 fusion.98
  150.5 2.7 %bitcast_reduce_fusion.2 = (f32[4,256]{1,0:T(4,128)S(1)}, f32[512,256,4]{1,0,2:T(8,128)}) fusion(bf16[256,1,4,128]{3,0,2,1:T(8,128)(2,1)S(1)} %get-tuple-element.193, bf16[4,512,1,128]{3,1,2,0:T(8,128)(2,1)} %get-tuple-element.192, s32[]{:T(128)} %get-tuple-element.179), kind=kOutput, calls=%fused_computation.1.clone.1 | convolution fusion | flops 135265280 | bytes 2494976 | tf_op jit(solution)/shard_map/while/body/eval_jaxpr/pkgd,skd->kgps/dot_general | solution.py:98
  153.3 3.2 %fusion.99 = f32[1,4,256,128]{3,2,1,0:T(8,128)} fusion(f32[512,256,4]{1,0,2:T(8,128)} %get-tuple-element.168, f32[4,256]{1,0:T(4,128)S(1)} %bitcast.95, f32[1,4,256,128]{3,2,1,0:T(8,128)} %get-tuple-element.182, f32[4,256]{1,0:T(4,128)S(1)} %get-tuple-element.169, pred[]{:T(512)S(6)} %compare.3, bf16[4,512,1,128]{3,1,2,0:T(8,128)(2,1)} %get-tuple-element.194, ...), kind=kOutput, calls=%fused_computation.6.clone.1 | convolution fusion | flops 136183808 | bytes 3285505 | tf_op jit(solution)/shard_map/while/body/eval_jaxpr/kgps,skd->kgpd/dot_general | solution.py:105
  156.5 0.4 fusion.98
  156.9 2.7 %bitcast_reduce_fusion.2 = (f32[4,256]{1,0:T(4,128)S(1)}, f32[512,256,4]{1,0,2:T(8,128)}) fusion(bf16[256,1,4,128]{3,0,2,1:T(8,128)(2,1)S(1)} %get-tuple-element.193, bf16[4,512,1,128]{3,1,2,0:T(8,128)(2,1)} %get-tuple-element.192, s32[]{:T(128)} %get-tuple-element.179), kind=kOutput, calls=%fused_computation.1.clone.1 | convolution fusion | flops 135265280 | bytes 2494976 | tf_op jit(solution)/shard_map/while/body/eval_jaxpr/pkgd,skd->kgps/dot_general | solution.py:98
  159.6 3.2 %fusion.99 = f32[1,4,256,128]{3,2,1,0:T(8,128)} fusion(f32[512,256,4]{1,0,2:T(8,128)} %get-tuple-element.168, f32[4,256]{1,0:T(4,128)S(1)} %bitcast.95, f32[1,4,256,128]{3,2,1,0:T(8,128)} %get-tuple-element.182, f32[4,256]{1,0:T(4,128)S(1)} %get-tuple-element.169, pred[]{:T(512)S(6)} %compare.3, bf16[4,512,1,128]{3,1,2,0:T(8,128)(2,1)} %get-tuple-element.194, ...), kind=kOutput, calls=%fused_computation.6.clone.1 | convolution fusion | flops 136183808 | bytes 3285505 | tf_op jit(solution)/shard_map/while/body/eval_jaxpr/kgps,skd->kgpd/dot_general | solution.py:105
  162.8 0.4 fusion.98
  163.2 2.7 %bitcast_reduce_fusion.2 = (f32[4,256]{1,0:T(4,128)S(1)}, f32[512,256,4]{1,0,2:T(8,128)}) fusion(bf16[256,1,4,128]{3,0,2,1:T(8,128)(2,1)S(1)} %get-tuple-element.193, bf16[4,512,1,128]{3,1,2,0:T(8,128)(2,1)} %get-tuple-element.192, s32[]{:T(128)} %get-tuple-element.179), kind=kOutput, calls=%fused_computation.1.clone.1 | convolution fusion | flops 135265280 | bytes 2494976 | tf_op jit(solution)/shard_map/while/body/eval_jaxpr/pkgd,skd->kgps/dot_general | solution.py:98
  165.9 3.2 %fusion.99 = f32[1,4,256,128]{3,2,1,0:T(8,128)} fusion(f32[512,256,4]{1,0,2:T(8,128)} %get-tuple-element.168, f32[4,256]{1,0:T(4,128)S(1)} %bitcast.95, f32[1,4,256,128]{3,2,1,0:T(8,128)} %get-tuple-element.182, f32[4,256]{1,0:T(4,128)S(1)} %get-tuple-element.169, pred[]{:T(512)S(6)} %compare.3, bf16[4,512,1,128]{3,1,2,0:T(8,128)(2,1)} %get-tuple-element.194, ...), kind=kOutput, calls=%fused_computation.6.clone.1 | convolution fusion | flops 136183808 | bytes 3285505 | tf_op jit(solution)/shard_map/while/body/eval_jaxpr/kgps,skd->kgpd/dot_general | solution.py:105
  169.1 0.4 fusion.98
  169.5 2.1 %copy.17 = f32[1,4,256,128]{2,3,1,0:T(8,128)} copy(f32[1,4,256,128]{3,2,1,0:T(8,128)} %get-tuple-element.43) | data formatting | bytes 1048576 | tf_op jit(solution)/shard_map/while | solution.py:128
  171.6 1.1 divide_convert_fusion
  172.7 1.5 convolution_convert_fusion
  174.2 9.8 %reduce-scatter.8.cloned.1.call-done = bf16[256,768]{1,0:T(8,128)(2,1)} async-done(((bf16[256,1536]{1,0:T(8,128)(2,1)}), bf16[256,768]{1,0:T(8,128)(2,1)}) %reduce-scatter.8.cloned.1.call-update) | async-done | bytes 393232 | tf_op jit(solution)/shard_map/reduce_scatter | solution.py:132
  184.0 2.1 %add_convert_fusion = bf16[256,768]{1,0:T(8,128)(2,1)} fusion(bf16[256,768]{1,0:T(8,128)(2,1)} %reduce-scatter.8.cloned.1.call-done, f32[256,768]{1,0:T(8,128)} %reduce-scatter.6.cloned.1.call-done, f32[512,768]{1,0:T(8,128)S(1)} %get-tuple-element.112), kind=kLoop, calls=%fused_computation.80 | loop fusion | flops 786432 | bytes 2359296 | tf_op jit(solution)/shard_map/convert_element_type | solution.py:138
  (42 shorter events, 0.2 us)
Async XLA Ops:
  6.5 166.2 %copy-start = (bf16[512,1536]{1,0:T(8,128)(2,1)S(1)}, bf16[512,1536]{1,0:T(8,128)(2,1)}, u32[]{:S(2)}) copy-start(bf16[512,1536]{1,0:T(8,128)(2,1)} %param.17) | copy-start | bytes 4718596
  6.5 22.4 %copy-start.2 = (bf16[256,768]{1,0:T(8,128)(2,1)S(1)}, bf16[256,768]{1,0:T(8,128)(2,1)}, u32[]{:S(2)}) copy-start(bf16[256,768]{1,0:T(8,128)(2,1)} %param.10) | copy-start | bytes 1179652
  6.5 41.2 %reduce-scatter.4.cloned.1.call-start = ((), (), s32[]{:S(2)}) async-start(), calls=%async_computation.3 | async-start | bytes 4718592 | tf_op jit(solution)/shard_map/reduce_scatter | solution.py:41
  7.8 17.4 %collective-permute-start = (bf16[192,768]{1,0:T(8,128)(2,1)S(1)}, bf16[192,768]{1,0:T(8,128)(2,1)S(1)}, u32[]{:S(2)}, u32[]{:S(2)}) collective-permute-start(bf16[192,768]{1,0:T(8,128)(2,1)S(1)} %get-tuple-element.115), channel_id=1, source_target_pairs={{0,2},{2,4},{4,6},{6,8},{8,10},{10,12},{12,14},{1,3},{3,5},{5,7},{... | collective-permute-start | bytes 884744 | tf_op jit(solution)/shard_map/ppermute | solution.py:18
  12.7 12.6 %collective-permute-start.1 = (bf16[192,768]{1,0:T(8,128)(2,1)S(1)}, bf16[192,768]{1,0:T(8,128)(2,1)S(1)}, u32[]{:S(2)}, u32[]{:S(2)}) collective-permute-start(bf16[192,768]{1,0:T(8,128)(2,1)S(1)} %get-tuple-element.116), channel_id=1, source_target_pairs={{2,0},{4,2},{6,4},{8,6},{10,8},{12,10},{14,12},{3,1},{5,3},{7,5},{... | collective-permute-start | bytes 884744 | tf_op jit(solution)/shard_map/ppermute | solution.py:19
  34.6 32.4 %reduce-scatter.6.cloned.1.call-start = ((), (), s32[]{:S(2)}) async-start(), calls=%async_computation.4 | async-start | bytes 2359296 | tf_op jit(solution)/shard_map/reduce_scatter | solution.py:41
  56.6 14.2 %copy-start.3 = (f32[768]{0:T(1024)S(1)}, f32[768]{0:T(1024)}, u32[]{:S(2)}) copy-start(f32[768]{0:T(1024)} %param.14) | copy-start | bytes 9220
  56.6 127.4 %reduce-scatter.8.cloned.1.call-start = ((), (), s32[]{:S(2)}) async-start(), calls=%async_computation.5 | async-start | bytes 1179648 | tf_op jit(solution)/shard_map/reduce_scatter | solution.py:132
  70.8 3.7 %copy-start.5 = (bf16[1536,2,128]{2,1,0:T(2,128)(2,1)S(1)}, bf16[1536,2,128]{2,1,0:T(2,128)(2,1)}, u32[]{:S(2)}) copy-start(bf16[1536,2,128]{2,1,0:T(2,128)(2,1)} %param.16) | copy-start | bytes 2359300
  74.5 67.5 %copy-start.4 = (bf16[1536,512]{1,0:T(8,128)(2,1)S(1)}, bf16[1536,512]{1,0:T(8,128)(2,1)}, u32[]{:S(2)}) copy-start(bf16[1536,512]{1,0:T(8,128)(2,1)} %param.15) | copy-start | bytes 4718596
  147.0 3.1 %copy-start.1 = (f32[512,256,4]{1,0,2:T(8,128)S(1)}, f32[512,256,4]{1,0,2:T(8,128)}, u32[]{:S(2)}) copy-start(f32[512,256,4]{1,0,2:T(8,128)} %get-tuple-element.168) | copy-start | bytes 6291460 | tf_op jit(solution)/shard_map/while
  153.3 3.2 %copy-start.1 = (f32[512,256,4]{1,0,2:T(8,128)S(1)}, f32[512,256,4]{1,0,2:T(8,128)}, u32[]{:S(2)}) copy-start(f32[512,256,4]{1,0,2:T(8,128)} %get-tuple-element.168) | copy-start | bytes 6291460 | tf_op jit(solution)/shard_map/while
  159.6 3.2 %copy-start.1 = (f32[512,256,4]{1,0,2:T(8,128)S(1)}, f32[512,256,4]{1,0,2:T(8,128)}, u32[]{:S(2)}) copy-start(f32[512,256,4]{1,0,2:T(8,128)} %get-tuple-element.168) | copy-start | bytes 6291460 | tf_op jit(solution)/shard_map/while
  165.9 3.2 %copy-start.1 = (f32[512,256,4]{1,0,2:T(8,128)S(1)}, f32[512,256,4]{1,0,2:T(8,128)}, u32[]{:S(2)}) copy-start(f32[512,256,4]{1,0,2:T(8,128)} %get-tuple-element.168) | copy-start | bytes 6291460 | tf_op jit(solution)/shard_map/while
Sparse Core Ops, SparseCore 0:
  34.7 13.0 reduce-scatter.3
  56.7 10.2 reduce-scatter.5
  174.3 9.6 reduce-scatter.7
where the time goes:
time: 193 us
  blocking collectives  76.9 us (40%)
  waiting for transfers between devices  41.4 us (21%)
  matrix products  35.1 us (18%)
  between operations  13.2 us (7%)
  other arithmetic  12.8 us (7%)
  local copies, waits for them, and re-layouts  6.81 us (4%)
  starting transfers between devices  6.27 us (3%)
    all_gather x1, blocking collectives, local(): key_piece = lax.all_gather(keys_local, 'seq', axis=0, tiled=True)  33.7 us
    all_gather x1, blocking collectives, local(): value_piece = lax.all_gather(values_local, 'seq', axis=0, tiled=True)  33.4 us
    reduce_scatter x2, waiting for transfers between devices, channel_mix(): lax.psum_scatter(jnp.dot(gelu_output, weight, preferred_element_type=jnp....  22 us
    dot_general x4, matrix products, key_block(): jnp.einsum('kgps,skd->kgpd', probs.astype(jnp.bfloat16), value_part, pref...  12.7 us
    dot_general x4, matrix products, key_block(): jnp.einsum('pkgd,skd->kgps', query_grid, key_part, preferred_element_type...  10.8 us
    reduce_scatter x1, waiting for transfers between devices, local(): lax.psum_scatter(jnp.dot(attended, out_weight, preferred_element_type=jnp...  9.8 us
    ppermute x1, waiting for transfers between devices, extended(): before = lax.ppermute(last, axis, up)  9.54 us
    dot_general x2, matrix products, channel_mix(): jnp.dot(gelu_output, weight, preferred_element_type=jnp.float32)  9.19 us
  transfers between devices with their start and end apart: 5, of which 4 were waited for; matrix products, arithmetic and copies ran while one was open for 2% of the time, Pallas kernels for 0%

commit v1 on v0

--- a/solution.py
+++ b/solution.py
@@ -118,7 +118,15 @@
     )
     carry = initial
     key_piece = lax.all_gather(keys_local, "seq", axis=0, tiled=True)
-    value_piece = lax.all_gather(values_local, "seq", axis=0, tiled=True)
+    parts_n = lax.axis_size("seq")
+    series = [(dev, (dev + 1) % parts_n) for dev in range(parts_n)]
+    base_arr = [None] * parts_n
+    base_arr[parts_n - 1] = values_local
+    for dev_i in range(parts_n - 2, -1, -1):
+        base_arr[dev_i] = lax.ppermute(base_arr[dev_i + 1], "seq", series)
+    shaped = jnp.concatenate(base_arr, 0)
+    res = (lax.axis_index("seq") + 1) * values_local.shape[0]
+    value_piece = jnp.roll(shaped, res, 0)
     key_count = key_piece.shape[0]
     block_len = math.gcd(key_count, 512)
     blocks = (

time: 193 us -> 217 us (1.12)
  waiting for transfers between devices: 41.4 us -> 82.6 us
  blocking collectives: 76.9 us -> 43.1 us
  local copies, waits for them, and re-layouts: 6.81 us -> 18.8 us
    ppermute x0 -> x7, waiting for transfers between devices: none -> 44 us  [local(): base_arr[dev_i] = lax.ppermute(base_arr[dev_i + 1], 'seq', series)]
    all_gather x1 -> x0, blocking collectives: 33.4 us -> none  [local(): value_piece = lax.all_gather(values_local, 'seq', axis=0, tiled=True)]
    unnamed x11 -> x46, local copies, waits for them, and re-layouts: 1 us -> 12.2 us
    reduce_scatter x1, waiting for transfers between devices: 9.8 us -> 6.97 us  [local(): lax.psum_scatter(jnp.dot(attended, out_weight, preferred_element_type=jnp...]
  transfers between devices with their start and end apart: 5 -> 12, of which waited for: 4 -> 11; matrix products, arithmetic and copies ran while one was open for 2% -> 3% of each run, Pallas kernels for 0% -> 0%
where the time goes in v1:
time: 217 us; the launch traced here: 216 us
  waiting for transfers between devices  82.6 us (38%)
  blocking collectives  43.1 us (20%)
  matrix products  36.7 us (17%)
  local copies, waits for them, and re-layouts  18.8 us (9%)
  between operations  13.3 us (6%)
  other arithmetic  12.8 us (6%)
  starting transfers between devices  8.09 us (4%)
    ppermute x7, waiting for transfers between devices, local(): base_arr[dev_i] = lax.ppermute(base_arr[dev_i + 1], 'seq', series)  44 us
    all_gather x1, blocking collectives, local(): key_piece = lax.all_gather(keys_local, 'seq', axis=0, tiled=True)  33.3 us
    reduce_scatter x2, waiting for transfers between devices, channel_mix(): lax.psum_scatter(jnp.dot(gelu_output, weight, preferred_element_type=jnp....  22 us
    dot_general x4, matrix products, key_block(): jnp.einsum('kgps,skd->kgpd', probs.astype(jnp.bfloat16), value_part, pref...  12.7 us
    unnamed x46, local copies, waits for them, and re-layouts  12.2 us
    dot_general x4, matrix products, key_block(): jnp.einsum('pkgd,skd->kgps', query_grid, key_part, preferred_element_type...  10.8 us
    ppermute x1, waiting for transfers between devices, extended(): before = lax.ppermute(last, axis, up)  9.54 us
    dot_general x2, matrix products, channel_mix(): jnp.dot(gelu_output, weight, preferred_element_type=jnp.float32)  9.19 us
  transfers between devices with their start and end apart: 12, of which 11 were waited for; matrix products, arithmetic and copies ran while one was open for 3% of the time, Pallas kernels for 0%

profile of v1, /device:TPU:0, one launch (start us, length us, event | category | flops | bytes accessed | tf_op | source)
XLA Modules:
  0.0 215.6 jit_solution(14444836839319954009)
XLA Ops:
  6.5 1.2 fusion.83
  7.8 4.9 %collective-permute-start = (bf16[192,768]{1,0:T(8,128)(2,1)S(1)}, bf16[192,768]{1,0:T(8,128)(2,1)S(1)}, u32[]{:S(2)}, u32[]{:S(2)}) collective-permute-start(bf16[192,768]{1,0:T(8,128)(2,1)S(1)} %get-tuple-element.115), channel_id=1, source_target_pairs={{0,2},{2,4},{4,6},{6,8},{8,10},{10,12},{12,14},{1,3},{3,5},{5,7},{... | collective-permute-start | bytes 884744 | tf_op jit(solution)/shard_map/ppermute | solution.py:18
  12.7 1.3 collective-permute-start.1
  14.8 0.9 slice_reduce_fusion.4
  15.7 9.5 %collective-permute-done = bf16[192,768]{1,0:T(8,128)(2,1)S(1)} collective-permute-done((bf16[192,768]{1,0:T(8,128)(2,1)S(1)}, bf16[192,768]{1,0:T(8,128)(2,1)S(1)}, u32[]{:S(2)}, u32[]{:S(2)}) %collective-permute-start) | collective-permute-done | bytes 294944 | tf_op jit(solution)/shard_map/ppermute | solution.py:18
  25.2 1.3 multiply_reduce_fusion
  26.5 2.5 %psum.21 = f32[640]{0:T(1024)S(1)} all-reduce(f32[640]{0:T(1024)S(1)} %multiply_reduce_fusion), channel_id=1, replica_groups=mesh['grp'=2,'seq'=8,'ch'=2] {'ch'}, use_global_device_ids=true, to_apply=%region_1.0 | all-reduce | flops 640 | bytes 5120 | tf_op jit(solution)/shard_map/psum | solution.py:26
  29.2 5.3 %fusion.20 = f32[512,1536]{1,0:T(8,128)} fusion(bf16[2,768,1536]{2,1,0:T(8,128)(2,1)} %param.13, f32[640,768]{1,0:T(8,128)S(1)} %multiply_multiply_fusion.1, f32[768]{0:T(1024)S(1)} %get-tuple-element.86, f32[768]{0:T(1024)S(1)} %get-tuple-element.87, f32[768]{0:T(1024)S(1)} %get-tuple-element.88, f32[768]{0:T(1024)S(1)} %get-tuple-element.89, ...), kind=kOutput, calls=%fused_computation.29 | convolution fusion | flops 1215037440 | bytes 13389824 | tf_op jit(solution)/shard_map/dot_general | solution.py:42
  34.6 1.4 maximum_convert_fusion
  36.1 11.7 %reduce-scatter.4.cloned.1.call-done = f32[512,768]{1,0:T(8,128)} async-done(((f32[512,1536]{1,0:T(8,128)}), f32[512,768]{1,0:T(8,128)}) %reduce-scatter.4.cloned.1.call-update) | async-done | bytes 1572880 | tf_op jit(solution)/shard_map/reduce_scatter | solution.py:41
  47.8 2.2 %multiply_reduce_fusion.1 = (f32[512]{0:T(512)S(1)}, f32[512,768]{1,0:T(8,128)S(1)}) fusion(f32[512,768]{1,0:T(8,128)} %reduce-scatter.4.cloned.1.call-done, f32[640,768]{1,0:T(8,128)} %maximum_convert_fusion, pred[512]{0:T(512)(128)(4,1)S(1)} %fusion.73), kind=kLoop, calls=%fused_computation.55 | loop fusion | flops 1572352 | bytes 4721152 | tf_op jit(solution)/shard_map/reduce_sum | solution.py:26
  50.0 2.5 %psum.22 = f32[512]{0:T(512)S(1)} all-reduce(f32[512]{0:T(512)S(1)} %get-tuple-element.111), channel_id=1, replica_groups=mesh['grp'=2,'seq'=8,'ch'=2] {'ch'}, use_global_device_ids=true, to_apply=%region_4.5 | all-reduce | flops 512 | bytes 4096 | tf_op jit(solution)/shard_map/psum | solution.py:26
  52.7 3.9 %fusion.18 = f32[256,1536]{1,0:T(8,128)} fusion(bf16[2,768,1536]{2,1,0:T(8,128)(2,1)} %param.13, f32[512,768]{1,0:T(8,128)S(1)} %multiply_multiply_fusion.2, f32[768]{0:T(1024)S(1)} %get-tuple-element.91, f32[768]{0:T(1024)S(1)} %get-tuple-element.92, f32[768]{0:T(1024)S(1)} %get-tuple-element.84, f32[768]{0:T(1024)S(1)} %get-tuple-element.85, ...), kind=kOutput, calls=%fused_computation.27 | convolution fusion | flops 607518720 | bytes 7884800 | tf_op jit(solution)/shard_map/dot_general | solution.py:42
  56.7 10.3 %reduce-scatter.6.cloned.1.call-done = f32[256,768]{1,0:T(8,128)} async-done(((f32[256,1536]{1,0:T(8,128)}), f32[256,768]{1,0:T(8,128)}) %reduce-scatter.6.cloned.1.call-update) | async-done | bytes 786448 | tf_op jit(solution)/shard_map/reduce_scatter | solution.py:41
  67.0 1.3 multiply_reduce_fusion.2
  68.3 2.5 %psum.23 = f32[256]{0:T(256)S(1)} all-reduce(f32[256]{0:T(256)S(1)} %multiply_reduce_fusion.2), channel_id=1, replica_groups=mesh['grp'=2,'seq'=8,'ch'=2] {'ch'}, use_global_device_ids=true, to_apply=%region_7.8 | all-reduce | flops 256 | bytes 2048 | tf_op jit(solution)/shard_map/psum | solution.py:26
  70.8 1.3 multiply_convert_fusion
  72.1 2.4 %all_gather.6 = bf16[256,1536]{1,0:T(8,128)(2,1)S(1)} all-gather(bf16[256,768]{1,0:T(8,128)(2,1)S(1)} %multiply_convert_fusion), channel_id=1, replica_groups=mesh['grp'=2,'seq'=8,'ch'=2] {'ch'}, dimensions={1}, use_global_device_ids=true | all-gather | bytes 1179648 | tf_op jit(solution)/shard_map/all_gather | solution.py:77
  74.5 0.9 copy-done.3
  75.8 1.8 collective-permute-start.2
  77.6 5.3 %collective-permute-done.2 = bf16[256,128]{1,0:T(8,128)(2,1)S(1)} collective-permute-done((bf16[256,128]{1,0:T(8,128)(2,1)S(1)}, bf16[256,128]{1,0:T(8,128)(2,1)S(1)}, u32[]{:S(2)}, u32[]{:S(2)}) %collective-permute-start.2) | collective-permute-done | bytes 65568 | tf_op jit(solution)/shard_map/ppermute | solution.py:126
  83.5 7.0 %collective-permute-done.3 = bf16[256,128]{1,0:T(8,128)(2,1)S(1)} collective-permute-done((bf16[256,128]{1,0:T(8,128)(2,1)S(1)}, bf16[256,128]{1,0:T(8,128)(2,1)S(1)}, u32[]{:S(2)}, u32[]{:S(2)}) %collective-permute-start.3) | collective-permute-done | bytes 65568 | tf_op jit(solution)/shard_map/ppermute | solution.py:126
  91.1 7.0 %collective-permute-done.4 = bf16[256,128]{1,0:T(8,128)(2,1)S(1)} collective-permute-done((bf16[256,128]{1,0:T(8,128)(2,1)S(1)}, bf16[256,128]{1,0:T(8,128)(2,1)S(1)}, u32[]{:S(2)}, u32[]{:S(2)}) %collective-permute-start.4) | collective-permute-done | bytes 65568 | tf_op jit(solution)/shard_map/ppermute | solution.py:126
  98.7 7.0 %collective-permute-done.5 = bf16[256,128]{1,0:T(8,128)(2,1)S(1)} collective-permute-done((bf16[256,128]{1,0:T(8,128)(2,1)S(1)}, bf16[256,128]{1,0:T(8,128)(2,1)S(1)}, u32[]{:S(2)}, u32[]{:S(2)}) %collective-permute-start.5) | collective-permute-done | bytes 65568 | tf_op jit(solution)/shard_map/ppermute | solution.py:126
  106.3 7.0 %collective-permute-done.6 = bf16[256,128]{1,0:T(8,128)(2,1)S(1)} collective-permute-done((bf16[256,128]{1,0:T(8,128)(2,1)S(1)}, bf16[256,128]{1,0:T(8,128)(2,1)S(1)}, u32[]{:S(2)}, u32[]{:S(2)}) %collective-permute-start.6) | collective-permute-done | bytes 65568 | tf_op jit(solution)/shard_map/ppermute | solution.py:126
  113.2 7.6 %collective-permute-done.7 = bf16[256,128]{1,0:T(8,128)(2,1)} collective-permute-done((bf16[256,128]{1,0:T(8,128)(2,1)S(1)}, bf16[256,128]{1,0:T(8,128)(2,1)}, u32[]{:S(2)}, u32[]{:S(2)}) %collective-permute-start.7) | collective-permute-done | bytes 65568 | tf_op jit(solution)/shard_map/ppermute | solution.py:126
  120.8 2.2 %convolution_convert_fusion.1 = bf16[256,512]{1,0:T(8,128)(2,1)S(1)} fusion(bf16[256,1536]{1,0:T(8,128)(2,1)} %copy-done.3, bf16[1536,512]{1,0:T(8,128)(2,1)} %param.15), kind=kOutput, calls=%fused_computation.56 | convolution fusion | flops 402784256 | bytes 2621440 | tf_op jit(solution)/shard_map/dot_general | solution.py:78
  123.9 1.0 copy.14
  124.9 3.2 %collective-permute-done.8 = bf16[256,128]{1,0:T(8,128)(2,1)} collective-permute-done((bf16[256,128]{1,0:T(8,128)(2,1)}, bf16[256,128]{1,0:T(8,128)(2,1)}, u32[]{:S(2)}, u32[]{:S(2)}) %collective-permute-start.8) | collective-permute-done | bytes 65568 | tf_op jit(solution)/shard_map/ppermute | solution.py:126
  129.8 0.9 constant_dynamic-update-slice_fusion.13
  130.7 0.9 constant_dynamic-update-slice_fusion.12
  131.5 0.9 constant_dynamic-update-slice_fusion.11
  134.1 0.9 constant_dynamic-update-slice_fusion.7
  136.0 33.3 %all_gather.7 = bf16[2048,128]{1,0:T(8,128)(2,1)} all-gather(bf16[256,128]{1,0:T(8,128)(2,1)S(1)} %get-tuple-element.118), channel_id=1, replica_groups=mesh['grp'=2,'seq'=8,'ch'=2] {'seq'}, dimensions={0}, use_global_device_ids=true | all-gather | bytes 589824 | tf_op jit(solution)/shard_map/all_gather | solution.py:120
  170.1 25.2 %while.15 = (s32[]{:T(128)}, f32[1,4,256]{2,1,0:T(4,128)S(1)}, f32[1,4,256]{2,1,0:T(4,128)S(1)}, f32[1,4,256,128]{3,2,1,0:T(8,128)}, bf16[4,512,1,128]{3,1,2,0:T...) while((s32[]{:T(128)}, f32[1,4,256]{2,1,0:T(4,128)S(1)}, ...), condition=%wide.region_11.12_spmd.clone, body=%wide.region_8.11_spmd.clone.sunk | while | flops 273029120 | bytes 16319621 | solution.py:136
  170.1 2.7 %bitcast_reduce_fusion.2 = (f32[4,256]{1,0:T(4,128)S(1)}, f32[512,256,4]{1,0,2:T(8,128)}) fusion(bf16[256,1,4,128]{3,0,2,1:T(8,128)(2,1)S(1)} %get-tuple-element.193, bf16[4,512,1,128]{3,1,2,0:T(8,128)(2,1)} %get-tuple-element.192, s32[]{:T(128)} %get-tuple-element.179), kind=kOutput, calls=%fused_computation.1.clone.1 | convolution fusion | flops 135265280 | bytes 2494976 | tf_op jit(solution)/shard_map/while/body/eval_jaxpr/pkgd,skd->kgps/dot_general | solution.py:98
  172.8 3.1 %fusion.98 = f32[1,4,256,128]{3,2,1,0:T(8,128)} fusion(f32[512,256,4]{1,0,2:T(8,128)} %get-tuple-element.168, f32[4,256]{1,0:T(4,128)S(1)} %bitcast.93, f32[1,4,256,128]{3,2,1,0:T(8,128)} %get-tuple-element.182, f32[4,256]{1,0:T(4,128)S(1)} %get-tuple-element.169, pred[]{:T(512)S(6)} %compare.4, bf16[4,512,1,128]{3,1,2,0:T(8,128)(2,1)} %get-tuple-element.194, ...), kind=kOutput, calls=%fused_computation.6.clone.1 | convolution fusion | flops 136183808 | bytes 3285505 | tf_op jit(solution)/shard_map/while/body/eval_jaxpr/kgps,skd->kgpd/dot_general | solution.py:105
  176.3 2.7 %bitcast_reduce_fusion.2 = (f32[4,256]{1,0:T(4,128)S(1)}, f32[512,256,4]{1,0,2:T(8,128)}) fusion(bf16[256,1,4,128]{3,0,2,1:T(8,128)(2,1)S(1)} %get-tuple-element.193, bf16[4,512,1,128]{3,1,2,0:T(8,128)(2,1)} %get-tuple-element.192, s32[]{:T(128)} %get-tuple-element.179), kind=kOutput, calls=%fused_computation.1.clone.1 | convolution fusion | flops 135265280 | bytes 2494976 | tf_op jit(solution)/shard_map/while/body/eval_jaxpr/pkgd,skd->kgps/dot_general | solution.py:98
  179.0 3.2 %fusion.98 = f32[1,4,256,128]{3,2,1,0:T(8,128)} fusion(f32[512,256,4]{1,0,2:T(8,128)} %get-tuple-element.168, f32[4,256]{1,0:T(4,128)S(1)} %bitcast.93, f32[1,4,256,128]{3,2,1,0:T(8,128)} %get-tuple-element.182, f32[4,256]{1,0:T(4,128)S(1)} %get-tuple-element.169, pred[]{:T(512)S(6)} %compare.4, bf16[4,512,1,128]{3,1,2,0:T(8,128)(2,1)} %get-tuple-element.194, ...), kind=kOutput, calls=%fused_computation.6.clone.1 | convolution fusion | flops 136183808 | bytes 3285505 | tf_op jit(solution)/shard_map/while/body/eval_jaxpr/kgps,skd->kgpd/dot_general | solution.py:105
  182.6 2.7 %bitcast_reduce_fusion.2 = (f32[4,256]{1,0:T(4,128)S(1)}, f32[512,256,4]{1,0,2:T(8,128)}) fusion(bf16[256,1,4,128]{3,0,2,1:T(8,128)(2,1)S(1)} %get-tuple-element.193, bf16[4,512,1,128]{3,1,2,0:T(8,128)(2,1)} %get-tuple-element.192, s32[]{:T(128)} %get-tuple-element.179), kind=kOutput, calls=%fused_computation.1.clone.1 | convolution fusion | flops 135265280 | bytes 2494976 | tf_op jit(solution)/shard_map/while/body/eval_jaxpr/pkgd,skd->kgps/dot_general | solution.py:98
  185.4 3.2 %fusion.98 = f32[1,4,256,128]{3,2,1,0:T(8,128)} fusion(f32[512,256,4]{1,0,2:T(8,128)} %get-tuple-element.168, f32[4,256]{1,0:T(4,128)S(1)} %bitcast.93, f32[1,4,256,128]{3,2,1,0:T(8,128)} %get-tuple-element.182, f32[4,256]{1,0:T(4,128)S(1)} %get-tuple-element.169, pred[]{:T(512)S(6)} %compare.4, bf16[4,512,1,128]{3,1,2,0:T(8,128)(2,1)} %get-tuple-element.194, ...), kind=kOutput, calls=%fused_computation.6.clone.1 | convolution fusion | flops 136183808 | bytes 3285505 | tf_op jit(solution)/shard_map/while/body/eval_jaxpr/kgps,skd->kgpd/dot_general | solution.py:105
  189.0 2.7 %bitcast_reduce_fusion.2 = (f32[4,256]{1,0:T(4,128)S(1)}, f32[512,256,4]{1,0,2:T(8,128)}) fusion(bf16[256,1,4,128]{3,0,2,1:T(8,128)(2,1)S(1)} %get-tuple-element.193, bf16[4,512,1,128]{3,1,2,0:T(8,128)(2,1)} %get-tuple-element.192, s32[]{:T(128)} %get-tuple-element.179), kind=kOutput, calls=%fused_computation.1.clone.1 | convolution fusion | flops 135265280 | bytes 2494976 | tf_op jit(solution)/shard_map/while/body/eval_jaxpr/pkgd,skd->kgps/dot_general | solution.py:98
  191.7 3.2 %fusion.98 = f32[1,4,256,128]{3,2,1,0:T(8,128)} fusion(f32[512,256,4]{1,0,2:T(8,128)} %get-tuple-element.168, f32[4,256]{1,0:T(4,128)S(1)} %bitcast.93, f32[1,4,256,128]{3,2,1,0:T(8,128)} %get-tuple-element.182, f32[4,256]{1,0:T(4,128)S(1)} %get-tuple-element.169, pred[]{:T(512)S(6)} %compare.4, bf16[4,512,1,128]{3,1,2,0:T(8,128)(2,1)} %get-tuple-element.194, ...), kind=kOutput, calls=%fused_computation.6.clone.1 | convolution fusion | flops 136183808 | bytes 3285505 | tf_op jit(solution)/shard_map/while/body/eval_jaxpr/kgps,skd->kgpd/dot_general | solution.py:105
  195.3 2.1 copy.15
  197.4 1.1 divide_convert_fusion
  198.4 1.5 convolution_convert_fusion
  199.9 7.0 %reduce-scatter.8.cloned.1.call-done = bf16[256,768]{1,0:T(8,128)(2,1)} async-done(((bf16[256,1536]{1,0:T(8,128)(2,1)}), bf16[256,768]{1,0:T(8,128)(2,1)}) %reduce-scatter.8.cloned.1.call-update) | async-done | bytes 393232 | tf_op jit(solution)/shard_map/reduce_scatter | solution.py:140
  206.9 2.1 add_convert_fusion
  (92 shorter events, 11.9 us)
Async XLA Ops:
  6.5 191.9 %copy-start = (bf16[512,1536]{1,0:T(8,128)(2,1)S(1)}, bf16[512,1536]{1,0:T(8,128)(2,1)}, u32[]{:S(2)}) copy-start(bf16[512,1536]{1,0:T(8,128)(2,1)} %param.17) | copy-start | bytes 4718596
  6.5 22.4 %copy-start.2 = (bf16[256,768]{1,0:T(8,128)(2,1)S(1)}, bf16[256,768]{1,0:T(8,128)(2,1)}, u32[]{:S(2)}) copy-start(bf16[256,768]{1,0:T(8,128)(2,1)} %param.10) | copy-start | bytes 1179652
  6.5 41.2 %reduce-scatter.4.cloned.1.call-start = ((), (), s32[]{:S(2)}) async-start(), calls=%async_computation.3 | async-start | bytes 4718592 | tf_op jit(solution)/shard_map/reduce_scatter | solution.py:41
  7.8 17.4 %collective-permute-start = (bf16[192,768]{1,0:T(8,128)(2,1)S(1)}, bf16[192,768]{1,0:T(8,128)(2,1)S(1)}, u32[]{:S(2)}, u32[]{:S(2)}) collective-permute-start(bf16[192,768]{1,0:T(8,128)(2,1)S(1)} %get-tuple-element.115), channel_id=1, source_target_pairs={{0,2},{2,4},{4,6},{6,8},{8,10},{10,12},{12,14},{1,3},{3,5},{5,7},{... | collective-permute-start | bytes 884744 | tf_op jit(solution)/shard_map/ppermute | solution.py:18
  12.7 12.6 %collective-permute-start.1 = (bf16[192,768]{1,0:T(8,128)(2,1)S(1)}, bf16[192,768]{1,0:T(8,128)(2,1)S(1)}, u32[]{:S(2)}, u32[]{:S(2)}) collective-permute-start(bf16[192,768]{1,0:T(8,128)(2,1)S(1)} %get-tuple-element.116), channel_id=1, source_target_pairs={{2,0},{4,2},{6,4},{8,6},{10,8},{12,10},{14,12},{3,1},{5,3},{7,5},{... | collective-permute-start | bytes 884744 | tf_op jit(solution)/shard_map/ppermute | solution.py:19
  34.6 32.4 %reduce-scatter.6.cloned.1.call-start = ((), (), s32[]{:S(2)}) async-start(), calls=%async_computation.4 | async-start | bytes 2359296 | tf_op jit(solution)/shard_map/reduce_scatter | solution.py:41
  56.6 14.2 %copy-start.14 = (f32[768]{0:T(1024)S(1)}, f32[768]{0:T(1024)}, u32[]{:S(2)}) copy-start(f32[768]{0:T(1024)} %param.14) | copy-start | bytes 9220
  56.6 150.3 %reduce-scatter.8.cloned.1.call-start = ((), (), s32[]{:S(2)}) async-start(), calls=%async_computation.5 | async-start | bytes 1179648 | tf_op jit(solution)/shard_map/reduce_scatter | solution.py:140
  70.8 4.6 %copy-start.15 = (bf16[1536,2,128]{2,1,0:T(2,128)(2,1)S(1)}, bf16[1536,2,128]{2,1,0:T(2,128)(2,1)}, u32[]{:S(2)}) copy-start(bf16[1536,2,128]{2,1,0:T(2,128)(2,1)} %param.16) | copy-start | bytes 2359300
  74.5 0.9 copy-start.3
  75.8 7.1 %collective-permute-start.2 = (bf16[256,128]{1,0:T(8,128)(2,1)S(1)}, bf16[256,128]{1,0:T(8,128)(2,1)S(1)}, u32[]{:S(2)}, u32[]{:S(2)}) collective-permute-start(bf16[256,128]{1,0:T(8,128)(2,1)S(1)} %slice.155), channel_id=1, source_target_pairs={{0,2},{2,4},{4,6},{6,8},{8,10},{10,12},{12,14},{14,0},{1,3},{3,5},... | collective-permute-start | bytes 196616 | tf_op jit(solution)/shard_map/ppermute | solution.py:126
  82.9 0.6 copy-start.4
  83.5 7.0 %collective-permute-start.3 = (bf16[256,128]{1,0:T(8,128)(2,1)S(1)}, bf16[256,128]{1,0:T(8,128)(2,1)S(1)}, u32[]{:S(2)}, u32[]{:S(2)}) collective-permute-start(bf16[256,128]{1,0:T(8,128)(2,1)S(1)} %collective-permute-done.2), channel_id=1, source_target_pairs={{0,2},{2,4},{4,6},{6,8},{8,10},{10,12},{12,14},{14,0},{1,3},{3,5},... | collective-permute-start | bytes 196616 | tf_op jit(solution)/shard_map/ppermute | solution.py:126
  90.5 0.6 copy-start.6
  91.1 7.0 %collective-permute-start.4 = (bf16[256,128]{1,0:T(8,128)(2,1)S(1)}, bf16[256,128]{1,0:T(8,128)(2,1)S(1)}, u32[]{:S(2)}, u32[]{:S(2)}) collective-permute-start(bf16[256,128]{1,0:T(8,128)(2,1)S(1)} %collective-permute-done.3), channel_id=1, source_target_pairs={{0,2},{2,4},{4,6},{6,8},{8,10},{10,12},{12,14},{14,0},{1,3},{3,5},... | collective-permute-start | bytes 196616 | tf_op jit(solution)/shard_map/ppermute | solution.py:126
  98.1 0.6 copy-start.8
  98.7 7.0 %collective-permute-start.5 = (bf16[256,128]{1,0:T(8,128)(2,1)S(1)}, bf16[256,128]{1,0:T(8,128)(2,1)S(1)}, u32[]{:S(2)}, u32[]{:S(2)}) collective-permute-start(bf16[256,128]{1,0:T(8,128)(2,1)S(1)} %collective-permute-done.4), channel_id=1, source_target_pairs={{0,2},{2,4},{4,6},{6,8},{8,10},{10,12},{12,14},{14,0},{1,3},{3,5},... | collective-permute-start | bytes 196616 | tf_op jit(solution)/shard_map/ppermute | solution.py:126
  105.6 0.6 copy-start.10
  106.3 7.0 %collective-permute-start.6 = (bf16[256,128]{1,0:T(8,128)(2,1)S(1)}, bf16[256,128]{1,0:T(8,128)(2,1)S(1)}, u32[]{:S(2)}, u32[]{:S(2)}) collective-permute-start(bf16[256,128]{1,0:T(8,128)(2,1)S(1)} %collective-permute-done.5), channel_id=1, source_target_pairs={{0,2},{2,4},{4,6},{6,8},{8,10},{10,12},{12,14},{14,0},{1,3},{3,5},... | collective-permute-start | bytes 196616 | tf_op jit(solution)/shard_map/ppermute | solution.py:126
  113.2 7.6 %copy-start.12 = (bf16[256,128]{1,0:T(8,128)(2,1)}, bf16[256,128]{1,0:T(8,128)(2,1)S(1)}, u32[]{:S(2)}) copy-start(bf16[256,128]{1,0:T(8,128)(2,1)S(1)} %collective-permute-done.6) | copy-start | bytes 196612
  113.2 7.6 %collective-permute-start.7 = (bf16[256,128]{1,0:T(8,128)(2,1)S(1)}, bf16[256,128]{1,0:T(8,128)(2,1)}, u32[]{:S(2)}, u32[]{:S(2)}) collective-permute-start(bf16[256,128]{1,0:T(8,128)(2,1)S(1)} %collective-permute-done.6), channel_id=1, source_target_pairs={{0,2},{2,4},{4,6},{6,8},{8,10},{10,12},{12,14},{14,0},{1,3},{3,5},... | collective-permute-start | bytes 196616 | tf_op jit(solution)/shard_map/ppermute | solution.py:126
  120.8 7.3 %collective-permute-start.8 = (bf16[256,128]{1,0:T(8,128)(2,1)}, bf16[256,128]{1,0:T(8,128)(2,1)}, u32[]{:S(2)}, u32[]{:S(2)}) collective-permute-start(bf16[256,128]{1,0:T(8,128)(2,1)} %collective-permute-done.7), channel_id=1, source_target_pairs={{0,2},{2,4},{4,6},{6,8},{8,10},{10,12},{12,14},{14,0},{1,3},{3,5},... | collective-permute-start | bytes 196616 | tf_op jit(solution)/shard_map/ppermute | solution.py:126
  123.8 12.0 %copy-start.13 = (bf16[256,128]{1,0:T(8,128)(2,1)S(1)}, bf16[256,128]{1,0:T(8,128)(2,1)}, u32[]{:S(2)}) copy-start(bf16[256,128]{1,0:T(8,128)(2,1)} %copy-done.12) | copy-start | bytes 196612
  123.8 12.0 %copy-start.11 = (bf16[256,128]{1,0:T(8,128)(2,1)S(1)}, bf16[256,128]{1,0:T(8,128)(2,1)}, u32[]{:S(2)}) copy-start(bf16[256,128]{1,0:T(8,128)(2,1)} %copy-done.10) | copy-start | bytes 196612
  123.9 12.0 %copy-start.9 = (bf16[256,128]{1,0:T(8,128)(2,1)S(1)}, bf16[256,128]{1,0:T(8,128)(2,1)}, u32[]{:S(2)}) copy-start(bf16[256,128]{1,0:T(8,128)(2,1)} %copy-done.8) | copy-start | bytes 196612
  123.9 12.0 %copy-start.7 = (bf16[256,128]{1,0:T(8,128)(2,1)S(1)}, bf16[256,128]{1,0:T(8,128)(2,1)}, u32[]{:S(2)}) copy-start(bf16[256,128]{1,0:T(8,128)(2,1)} %copy-done.6) | copy-start | bytes 196612
  123.9 12.1 %copy-start.5 = (bf16[256,128]{1,0:T(8,128)(2,1)S(1)}, bf16[256,128]{1,0:T(8,128)(2,1)}, u32[]{:S(2)}) copy-start(bf16[256,128]{1,0:T(8,128)(2,1)} %copy-done.4) | copy-start | bytes 196612
  172.8 3.1 %copy-start.1 = (f32[512,256,4]{1,0,2:T(8,128)S(1)}, f32[512,256,4]{1,0,2:T(8,128)}, u32[]{:S(2)}) copy-start(f32[512,256,4]{1,0,2:T(8,128)} %get-tuple-element.168) | copy-start | bytes 6291460 | tf_op jit(solution)/shard_map/while
  179.0 3.2 %copy-start.1 = (f32[512,256,4]{1,0,2:T(8,128)S(1)}, f32[512,256,4]{1,0,2:T(8,128)}, u32[]{:S(2)}) copy-start(f32[512,256,4]{1,0,2:T(8,128)} %get-tuple-element.168) | copy-start | bytes 6291460 | tf_op jit(solution)/shard_map/while
  185.3 3.2 %copy-start.1 = (f32[512,256,4]{1,0,2:T(8,128)S(1)}, f32[512,256,4]{1,0,2:T(8,128)}, u32[]{:S(2)}) copy-start(f32[512,256,4]{1,0,2:T(8,128)} %get-tuple-element.168) | copy-start | bytes 6291460 | tf_op jit(solution)/shard_map/while
  191.7 3.2 %copy-start.1 = (f32[512,256,4]{1,0,2:T(8,128)S(1)}, f32[512,256,4]{1,0,2:T(8,128)}, u32[]{:S(2)}) copy-start(f32[512,256,4]{1,0,2:T(8,128)} %get-tuple-element.168) | copy-start | bytes 6291460 | tf_op jit(solution)/shard_map/while
Sparse Core Ops, SparseCore 0:
  34.7 13.0 reduce-scatter.3
  56.7 10.2 reduce-scatter.5
  200.1 6.8 reduce-scatter.7
